TPU v7x, 32 devices: a whole 2x2x4 slice. The times are simulated.
32 devices in a mesh: dp: 4 (over y, x), vocab: 8 (over z, core).
Axes of the slice: x: 2, y: 2, z: 4, core: 2. Of those that a mesh axis runs over, the one named last changes fastest.
Arguments:
- token_ids: int32 [64, 512], P(('dp', 'vocab')), may hold values from 0 to 30719, as said below
- type_ids: int32 [64, 512], P(('dp', 'vocab')), may hold values from 0 to 1
- lengths: int32 [64], P(('dp', 'vocab')), may hold values from 20 to 512, as said below
- word_table: bfloat16 [30720, 768], P('vocab'), may hold values from -6 to 6
- pos_table: bfloat16 [512, 768], replicated, may hold values from -4 to 4
- token_type_embeddings: bfloat16 [2, 768], replicated, may hold values from -4 to 4
- emb_gain: float32 [768], replicated, may hold values from 0.25 to 1.75
- emb_bias: float32 [768], replicated, may hold values from -3 to 3
- query_weight: bfloat16 [768, 768], replicated, may hold values from -0.21875 to 0.21875
- query_bias: float32 [768], replicated, may hold values from -3 to 3
- key_weight: bfloat16 [768, 768], replicated, may hold values from -0.21875 to 0.21875
- value_weight: bfloat16 [768, 768], replicated, may hold values from -0.21875 to 0.21875
- value_bias: float32 [768], replicated, may hold values from -3 to 3
- out_weight: bfloat16 [768, 768], replicated, may hold values from -0.875 to 0.875
- out_bias: float32 [768], replicated, may hold values from -3 to 3
- attn_gain: float32 [768], replicated, may hold values from 0.25 to 1.75
- attn_bias: float32 [768], replicated, may hold values from -3 to 3
- up_weight: bfloat16 [768, 3072], replicated, may hold values from -0.21875 to 0.21875
- up_bias: float32 [3072], replicated, may hold values from -3 to 3
- down_weight: bfloat16 [3072, 768], replicated, may hold values from -0.109375 to 0.109375
- down_bias: float32 [768], replicated, may hold values from -3 to 3
- final_gain: float32 [768], replicated, may hold values from 0.25 to 1.75
- final_bias: float32 [768], replicated, may hold values from -3 to 3
- cotangent: bfloat16 [64, 512, 768], P(('dp', 'vocab')), may hold values from -6 to 6
Outputs:
- encoded: float32 [64, 512, 768], P(('dp', 'vocab'))
- word_grad: float32 [30720, 768], P('vocab')
- pos_grad: float32 [512, 768], P('vocab')
- type_grad: float32 [2, 768], P(None, 'vocab')
- emb_gain_grad: float32 [768], P('vocab')
- emb_bias_grad: float32 [768], P('vocab')
- query_weight_grad: float32 [768, 768], P('vocab')
- query_bias_grad: float32 [768], P('vocab')
- key_weight_grad: float32 [768, 768], P('vocab')
- value_weight_grad: float32 [768, 768], P('vocab')
- value_bias_grad: float32 [768], P('vocab')
- out_weight_grad: float32 [768, 768], P('vocab')
- out_bias_grad: float32 [768], P('vocab')
- attn_gain_grad: float32 [768], P('vocab')
- attn_bias_grad: float32 [768], P('vocab')
- up_weight_grad: float32 [768, 3072], P('vocab')
- up_bias_grad: float32 [3072], P('vocab')
- down_weight_grad: float32 [3072, 768], P('vocab')
- down_bias_grad: float32 [768], P('vocab')
- final_gain_grad: float32 [768], P('vocab')
- final_bias_grad: float32 [768], P('vocab')
Inputs may be any that keep to these rules, and one draw needn't show every extreme that they name: `token_ids`: among the tokens of one device, at most 256 ids fall into the 3840 rows of word_table that one index of vocab holds; for one such block of rows, the same on every device, exactly 256 do. `lengths`: the tokens at positions from a sequence's length on are padding; some sequence has length 512 and some 20.
All inputs are finite; a program needn't handle non-finite values.
Results may differ from a plain program's by a relative error of at most 0.017.
Values may be sent and summed in bfloat16 or wider, within the bound.
A program may use at most 192 MiB of HBM per device.

v0:
```python
from functools import partial
import jax
import jax.numpy as jnp
from jax import lax
from jax.sharding import PartitionSpec as P

HEADS = 12
HEAD = 64
L = 512
EPSILON = 1e-12


def layer_norm(values, gain, bias):
    center = values - jnp.mean(values, -1, keepdims=True)
    spread = jnp.mean(center * center, -1, keepdims=True)
    return center * lax.rsqrt(spread + EPSILON) * gain + bias


def matmul(left, right):
    return jnp.dot(left, right, preferred_element_type=jnp.float32)


def matmul_tn(left, right):
    return lax.dot_general(
        left, right, (((0,), (0,)), ((), ())), preferred_element_type=jnp.float32
    )


def matmul_nt(left, right):
    return lax.dot_general(
        left, right, (((1,), (1,)), ((), ())), preferred_element_type=jnp.float32
    )


def masked_scores(query, keys, length):
    scores = jnp.einsum("qhd,khd->hqk", query, keys, preferred_element_type=jnp.float32) * HEAD ** (
        -0.5
    )
    visible = jnp.arange(L) < length
    return jnp.where(visible[None, None, :], scores, -1000000000.0)


def attend_forward(block):
    query, keys, values, length = block
    scores = masked_scores(query, keys, length)
    highest = jnp.max(scores, -1, keepdims=True)
    expd = jnp.exp(scores - highest)
    totals = jnp.sum(expd, -1, keepdims=True)
    probs_low = (expd / totals).astype(jnp.bfloat16)
    mixed = jnp.einsum("hqk,khd->qhd", probs_low, values, preferred_element_type=jnp.float32)
    return (mixed.astype(jnp.bfloat16), highest + jnp.log(totals))


def attend_backward(block):
    query, keys, values, grad_mixed, logsum, length = block
    probs = jnp.exp(masked_scores(query, keys, length) - logsum)
    probs_low = probs.astype(jnp.bfloat16)
    grad_values = jnp.einsum(
        "hqk,qhd->khd", probs_low, grad_mixed, preferred_element_type=jnp.float32
    )
    grad_probs = jnp.einsum("qhd,khd->hqk", grad_mixed, values, preferred_element_type=jnp.float32)
    inner = jnp.sum(grad_probs * probs, -1, keepdims=True)
    grad_scores = (probs * (grad_probs - inner)).astype(jnp.bfloat16)
    scale = HEAD ** (-0.5)
    grad_query = (
        jnp.einsum("hqk,khd->qhd", grad_scores, keys, preferred_element_type=jnp.float32) * scale
    )
    grad_keys = (
        jnp.einsum("hqk,qhd->khd", grad_scores, query, preferred_element_type=jnp.float32) * scale
    )
    return (grad_query, grad_keys, grad_values)


def swap(value, axis_name, bit):
    size = lax.axis_size(axis_name)
    return lax.ppermute(value, axis_name, [(i, i ^ bit) for i in range(size)])


def pick(value, index, axis):
    return lax.dynamic_index_in_dim(value, index, axis, keepdims=False)


def plus(left, right):
    return (left.astype(jnp.float32) + right.astype(jnp.float32)).astype(jnp.bfloat16)


def dp_bits():
    index = lax.axis_index("dp")
    return (lax.rem(index, 2), index // 2)


def reorder(own, across_x, across_y, across_both):
    xb, yb = dp_bits()
    flip_x, flip_y = (xb == 1, yb == 1)
    rows = [[own, across_y], [across_x, across_both]]
    rows = [[jnp.where(flip_x, rows[1 - i][j], rows[i][j]) for j in range(2)] for i in range(2)]
    rows = [[jnp.where(flip_y, rows[i][1 - j], rows[i][j]) for j in range(2)] for i in range(2)]
    return rows


def sum_over_all(grad):
    size = lax.axis_size("vocab")
    me = lax.axis_index("vocab")
    core = lax.rem(me, 2)
    place = me // 2
    places = size // 2
    total, n = grad.shape
    r = total // size
    xb, yb = dp_bits()
    grad = grad.reshape(places, 2, r, n)
    other = swap(pick(grad, 1 - core, 1), "vocab", 1)
    held = plus(pick(grad, core, 1), other).reshape(places, 2, 2, r // 4, n)
    first, last = (held[: places // 2], held[places // 2 :])
    first_in = swap(pick(first, 1 - xb, 1), "dp", 1)
    last_in = swap(pick(last, 1 - yb, 2), "dp", 2)
    first = plus(pick(first, xb, 1), first_in)
    last = plus(pick(last, yb, 2), last_in)
    first_in = swap(pick(first, 1 - yb, 1), "dp", 2)
    last_in = swap(pick(last, 1 - xb, 1), "dp", 1)
    first = plus(pick(first, yb, 1), first_in)
    last = plus(pick(last, xb, 1), last_in)
    held = jnp.concatenate([first, last], 0)
    summed = pick(held, place, 0).astype(jnp.float32)
    for step in range(1, places):
        block = pick(held, lax.rem(place + step, places), 0)
        block = lax.ppermute(block, "vocab", [(i, (i + 2 * step) % size) for i in range(size)])
        summed = summed + block.astype(jnp.float32)
    own = summed.astype(jnp.bfloat16)
    across_x = swap(own, "dp", 1)
    across_y = swap(own, "dp", 2)
    half = n // 2
    both = jnp.concatenate(
        [swap(across_x[:, :half], "dp", 2), swap(across_y[:, half:], "dp", 1)], 1
    )
    rows = reorder(own, across_x, across_y, both)
    return (
        jnp.stack([rows[0][0], rows[0][1], rows[1][0], rows[1][1]])
        .reshape(r, n)
        .astype(jnp.float32)
    )


def sum_over_dp(grad):
    rows, n = grad.shape
    xb, yb = dp_bits()
    held = grad.reshape(2, 2, 2, rows // 8, n)
    first, last = (held[0], held[1])
    first_in = swap(pick(first, 1 - xb, 0), "dp", 1)
    last_in = swap(pick(last, 1 - yb, 1), "dp", 2)
    first = plus(pick(first, xb, 0), first_in)
    last = plus(pick(last, yb, 1), last_in)
    first_in = swap(pick(first, 1 - yb, 0), "dp", 2)
    last_in = swap(pick(last, 1 - xb, 0), "dp", 1)
    first = plus(pick(first, yb, 0), first_in)
    last = plus(pick(last, xb, 0), last_in)
    first_x = swap(first, "dp", 1)
    last_y = swap(last, "dp", 2)
    first_y = swap(jnp.stack([first, first_x]), "dp", 2)
    last_x = swap(jnp.stack([last, last_y]), "dp", 1)
    a = reorder(first, first_x, first_y[0], first_y[1])
    b = reorder(last, last_x[0], last_y, last_x[1])
    parts = [p for group in (a, b) for line in group for p in line]
    return jnp.concatenate(parts, 0).astype(jnp.float32)


def local(
    token_ids,
    type_ids,
    lengths,
    word_table,
    pos_table,
    token_type_embeddings,
    emb_gain,
    emb_bias,
    query_weight,
    query_bias,
    key_weight,
    value_weight,
    value_bias,
    out_weight,
    out_bias,
    attn_gain,
    attn_bias,
    up_weight,
    up_bias,
    down_weight,
    down_bias,
    final_gain,
    final_bias,
    cotangent,
):
    seq_count, seq_len = token_ids.shape
    tokens = seq_count * seq_len
    width = word_table.shape[1]
    rows_local = word_table.shape[0]
    owners = lax.axis_size("vocab")
    capacity = max(2, 2 * tokens // owners)
    flat_ids = token_ids.reshape(tokens)
    owner = flat_ids // rows_local
    member = (owner[:, None] == jnp.arange(owners)[None, :]).astype(jnp.int32)
    earlier = jnp.cumsum(member, 0) - member
    rank = jnp.sum(earlier * member, 1)
    slot = owner * capacity + rank
    requests = (
        jnp.full((owners * capacity,), -1, jnp.int32).at[slot].set(flat_ids - owner * rows_local)
    )
    requests = requests.reshape(owners, capacity)
    asked = lax.all_to_all(requests, "vocab", split_axis=0, concat_axis=0, tiled=True)
    valid = asked >= 0
    found = word_table[jnp.maximum(asked, 0)]
    found = jnp.where(valid[..., None], found, jnp.zeros((), jnp.bfloat16))
    returned = lax.all_to_all(found, "vocab", split_axis=0, concat_axis=0, tiled=True)
    word_rows = returned.reshape(owners * capacity, width)[slot]
    kinds = token_type_embeddings.shape[0]
    selection_matrix = (type_ids[..., None] == jnp.arange(kinds)[None, None, :]).astype(jnp.float32)
    type_rows = jnp.einsum(
        "tcr,rb->tcb",
        selection_matrix,
        token_type_embeddings.astype(jnp.float32),
        precision=lax.Precision.HIGHEST,
    )
    embedded = (
        word_rows.reshape(seq_count, seq_len, width).astype(jnp.float32)
        + pos_table.astype(jnp.float32)[None]
        + type_rows
    )
    normed = layer_norm(embedded, emb_gain, emb_bias).reshape(tokens, width)
    normed_low = normed.astype(jnp.bfloat16)
    query = (matmul(normed_low, query_weight) + query_bias).astype(jnp.bfloat16)
    keys = matmul(normed_low, key_weight).astype(jnp.bfloat16)
    values = (matmul(normed_low, value_weight) + value_bias).astype(jnp.bfloat16)
    split_shape = (seq_count, seq_len, HEADS, HEAD)
    query_split = query.reshape(split_shape)
    keys_split = keys.reshape(split_shape)
    values_split = values.reshape(split_shape)
    mixed, logsum = lax.map(attend_forward, (query_split, keys_split, values_split, lengths))
    mixed_low = mixed.reshape(tokens, width)
    first = normed + matmul(mixed_low, out_weight) + out_bias
    hidden = layer_norm(first, attn_gain, attn_bias)
    hidden_reduced_precision = hidden.astype(jnp.bfloat16)
    upper = matmul(hidden_reduced_precision, up_weight) + up_bias
    active_low = jax.nn.gelu(upper, approximate=False).astype(jnp.bfloat16)
    second = hidden + matmul(active_low, down_weight) + down_bias
    encoded = layer_norm(second, final_gain, final_bias)
    grad_out = cotangent.reshape(tokens, width).astype(jnp.float32)
    _, final_pull = jax.vjp(layer_norm, second, final_gain, final_bias)
    grad_second, grad_final_gain, grad_final_bias = final_pull(grad_out)
    grad_down_bias = jnp.sum(grad_second, 0)
    second_matmul_gradient_reduced = grad_second.astype(jnp.bfloat16)
    grad_down = matmul_tn(active_low, second_matmul_gradient_reduced)
    grad_active = matmul_nt(second_matmul_gradient_reduced, down_weight)
    _, gelu_pull = jax.vjp(partial(jax.nn.gelu, approximate=False), upper)
    (grad_upper,) = gelu_pull(grad_active)
    grad_up_bias = jnp.sum(grad_upper, 0)
    grad_upper_low = grad_upper.astype(jnp.bfloat16)
    grad_up = matmul_tn(hidden_reduced_precision, grad_upper_low)
    grad_hidden = grad_second + matmul_nt(grad_upper_low, up_weight)
    _, attn_pull = jax.vjp(layer_norm, first, attn_gain, attn_bias)
    grad_first, grad_attn_gain, grad_attn_bias = attn_pull(grad_hidden)
    grad_out_bias = jnp.sum(grad_first, 0)
    grad_first_low = grad_first.astype(jnp.bfloat16)
    grad_out_weight = matmul_tn(mixed_low, grad_first_low)
    grad_mixed = matmul_nt(grad_first_low, out_weight).astype(jnp.bfloat16)
    grad_query, grad_keys, grad_values = lax.map(
        attend_backward,
        (query_split, keys_split, values_split, grad_mixed.reshape(split_shape), logsum, lengths),
    )
    grad_query = grad_query.reshape(tokens, width)
    grad_keys = grad_keys.reshape(tokens, width)
    grad_values = grad_values.reshape(tokens, width)
    grad_query_bias = jnp.sum(grad_query, 0)
    grad_value_bias = jnp.sum(grad_values, 0)
    grad_query_low = grad_query.astype(jnp.bfloat16)
    grad_keys_low = grad_keys.astype(jnp.bfloat16)
    grad_values_low = grad_values.astype(jnp.bfloat16)
    grad_query_weight = matmul_tn(normed_low, grad_query_low)
    grad_key_weight = matmul_tn(normed_low, grad_keys_low)
    grad_value_weight = matmul_tn(normed_low, grad_values_low)
    grad_normed = (
        grad_first
        + matmul_nt(grad_query_low, query_weight)
        + matmul_nt(grad_keys_low, key_weight)
        + matmul_nt(grad_values_low, value_weight)
    )
    _, emb_pull = jax.vjp(layer_norm, embedded, emb_gain, emb_bias)
    embedding_output_gradient, grad_emb_gain, grad_emb_bias = emb_pull(
        grad_normed.reshape(seq_count, seq_len, width)
    )
    grad_pos = jnp.sum(embedding_output_gradient, 0)
    token_type_gradient = jnp.einsum(
        "nox,noh->xh", selection_matrix, embedding_output_gradient, precision=lax.Precision.HIGHEST
    )
    bf = jnp.bfloat16
    per = width // owners
    grad_down_all = sum_over_all(grad_down.astype(bf))
    grad_up_all = sum_over_all(grad_up.astype(bf))
    places = slot[None, :] == jnp.arange(owners * capacity)[:, None]
    outgoing = matmul(
        places.astype(bf), embedding_output_gradient.reshape(tokens, width).astype(bf)
    ).astype(bf)
    hits = (jnp.arange(rows_local)[:, None] == asked.reshape(-1)[None, :]).astype(bf)
    pieces = []
    step = 256
    for start in range(0, width, step):
        incoming = lax.all_to_all(
            outgoing[:, start : start + step].reshape(owners, capacity, step),
            "vocab",
            split_axis=0,
            concat_axis=0,
            tiled=True,
        )
        dense = matmul(hits, incoming.reshape(owners * capacity, step)).astype(bf)
        pieces.append(sum_over_dp(dense))
    grad_word = jnp.concatenate(pieces, 1)
    small = jnp.stack(
        [
            grad_query_bias,
            grad_value_bias,
            grad_out_bias,
            grad_attn_gain,
            grad_attn_bias,
            grad_emb_gain,
            grad_emb_bias,
            grad_down_bias,
            grad_final_gain,
            grad_final_bias,
            token_type_gradient[0],
            token_type_gradient[1],
        ]
    )
    small = small.reshape(12, owners, per).transpose(1, 0, 2).reshape(owners, 12 * per)
    small = jnp.concatenate([small, grad_up_bias.reshape(owners, 4 * per)], 1)
    wide = 4 * width
    lines = seq_len // owners * width // wide
    rest = per // 3 - lines
    small_lines = jnp.pad(small, ((0, 0), (0, rest * wide - 16 * per))).reshape(owners, rest, wide)
    mixed_grads = jnp.concatenate(
        [grad_query_weight, grad_key_weight, grad_value_weight, grad_out_weight], 1
    ).astype(bf)
    packed = jnp.concatenate(
        [
            mixed_grads.reshape(owners, per, wide),
            grad_pos.astype(bf).reshape(owners, lines, wide),
            small_lines.astype(bf),
        ],
        1,
    )
    packed = sum_over_all(packed.reshape(-1, wide))
    weights = packed[:per]
    grad_query_weight = weights[:, :width]
    grad_key_weight = weights[:, width : 2 * width]
    grad_value_weight = weights[:, 2 * width : 3 * width]
    grad_out_weight = weights[:, 3 * width :]
    grad_pos = packed[per : per + lines].reshape(seq_len // owners, width)
    small = packed[per + lines :].reshape(-1)[: 16 * per].reshape(16, per)
    (
        grad_query_bias,
        grad_value_bias,
        grad_out_bias,
        grad_attn_gain,
        grad_attn_bias,
        grad_emb_gain,
        grad_emb_bias,
        grad_down_bias,
        grad_final_gain,
        grad_final_bias,
    ) = [small[i] for i in range(10)]
    token_type_gradient = small[10:12]
    grad_up_bias = small[12:].reshape(-1)
    grad_up, grad_down = (grad_up_all, grad_down_all)
    return (
        encoded.reshape(seq_count, seq_len, width),
        grad_word,
        grad_pos,
        token_type_gradient,
        grad_emb_gain,
        grad_emb_bias,
        grad_query_weight,
        grad_query_bias,
        grad_key_weight,
        grad_value_weight,
        grad_value_bias,
        grad_out_weight,
        grad_out_bias,
        grad_attn_gain,
        grad_attn_bias,
        grad_up,
        grad_up_bias,
        grad_down,
        grad_down_bias,
        grad_final_gain,
        grad_final_bias,
    )


def solution(mesh):
    placed = (
        P(("dp", "vocab"), None),
        P(("dp", "vocab"), None),
        P(("dp", "vocab")),
        P("vocab", None),
        P(),
        P(),
        P(),
        P(),
        P(),
        P(),
        P(),
        P(),
        P(),
        P(),
        P(),
        P(),
        P(),
        P(),
        P(),
        P(),
        P(),
        P(),
        P(),
        P(("dp", "vocab"), None, None),
    )
    return jax.shard_map(
        local,
        mesh=mesh,
        in_specs=placed,
        out_specs=(
            P(("dp", "vocab"), None, None),
            P("vocab", None),
            P("vocab", None),
            P(None, "vocab"),
            P("vocab"),
            P("vocab"),
            P("vocab", None),
            P("vocab"),
            P("vocab", None),
            P("vocab", None),
            P("vocab"),
            P("vocab", None),
            P("vocab"),
            P("vocab"),
            P("vocab"),
            P("vocab", None),
            P("vocab"),
            P("vocab", None),
            P("vocab"),
            P("vocab"),
            P("vocab"),
        ),
        check_vma=False,
    )
```

profile of v0, /device:TPU:0, one launch (start us, length us, event | category | flops | bytes accessed | tf_op | source)
XLA Modules:
  0.0 785.7 jit_solution(7070408737902939160)
XLA Ops:
  12.1 11.7 %all_to_all.29 = s32[8,1,256]{2,1,0:T(1,128)S(1)} all-to-all(s32[8,1,256]{2,1,0:T(1,128)S(1)} %bitcast.728), channel_id=1, replica_groups=mesh['dp'=4,'vocab'=8] {'vocab'}, dimensions={0} | all-to-all | bytes 16384 | tf_op jit(solution)/shard_map/all_to_all | solution.py:208
  23.9 13.5 %gather_fusion = bf16[2048,768]{1,0:T(8,128)(2,1)} fusion(bf16[3840,768]{1,0:T(8,128)(2,1)} %param.31, s32[2048]{0:T(1024)S(1)} %broadcast_clamp_fusion), kind=kCustom, calls=%fused_computation | custom fusion | bytes 6299648 | tf_op jit(solution)/shard_map/gather | solution.py:210
  48.2 69.1 %all-to-all-done.1 = bf16[8,256,768]{2,1,0:T(8,128)(2,1)} async-done(((bf16[8,256,768]{2,1,0:T(8,128)(2,1)}), bf16[8,256,768]{2,1,0:T(8,128)(2,1)}, u32[]{:S(2)}, u32[]{:S(2)}) %all-to-all-start.1) | async-done | bytes 3145760 | tf_op jit(solution)/shard_map/all_to_all | solution.py:212
  117.3 8.0 %gather_fusion.1 = bf16[1024,768]{1,0:T(8,128)(2,1)} fusion(bf16[2048,768]{1,0:T(8,128)(2,1)} %bitcast.25, s32[1024]{0:T(1024)S(1)} %broadcast_clamp_fusion.1), kind=kCustom, calls=%fused_computation.1 | custom fusion | bytes 3149824 | tf_op jit(solution)/shard_map/gather | solution.py:213
  164.0 25.6 %while.26 = (s32[]{:T(128)}, bf16[2,512,12,64]{1,3,2,0:T(8,128)(2,1)}, f32[2,12,512,1]{2,1,3,0:T(8,128)}, bf16[2,512,12,64]{1,3,2,0:T(8,128)(2,1)}, s32[2]{0:T(1...) while((s32[]{:T(128)}, ...), condition=%wide.region_9.10_spmd, body=%wide.region_6.9_spmd.sunk | while | flops 843442688 | bytes 47411840 | solution.py:236
  198.1 35.1 %multiply_convert_fusion.1 = (bf16[1024,3072]{1,0:T(8,128)(2,1)S(1)}, f32[1024,3072]{1,0:T(8,128)}, f32[1024,3072]{1,0:T(8,128)}) fusion(f32[3072]{0:T(1024)S(1)} %copy-done.82, bf16[768,3072]{1,0:T(8,128)(2,1)S(1)} %bitcast.738, f32[1024,768]{1,0:T(8,128)S(1)} %get-tuple-element.331, f32[768]{0:T(1024)S(1)} %copy-done.87, f32[768]{0:T(1024)S(1)} %copy-done.73, ...), kind=kOutput, calls=%fused_computation.69 | convolution fusion | flops 5043388416 | bytes 39348224 | tf_op jit(solution)/shard_map/dot_general | solution.py:20
  244.9 7.7 convolution_convert_fusion
  252.6 19.4 %fusion.216 = (bf16[3072]{0:T(1024)(128)(2,1)}, bf16[1024,3072]{1,0:T(8,128)(2,1)}) fusion(f32[1024,3072]{1,0:T(8,128)} %get-tuple-element.251, bf16[3072,768]{1,0:T(8,128)(2,1)} %param.47, f32[1024,768]{1,0:T(8,128)} %copy-done.21, f32[1024]{0:T(1024)S(1)} %negate_multiply_fusion.3, f32[1024,3072]{1,0:T(8,128)} %get-tuple-element.332, f32[3072]{0:T(1024)S(1)} %copy-done.82), kind=kOutput, calls=%fused_computation.487 | convolution fusion | flops 4883739648 | bytes 39344128 | tf_op jit(solution)/shard_map/dot_general | solution.py:30
  272.1 10.7 %convolution_convert_fusion.1 = bf16[768,3072]{1,0:T(8,128)(2,1)} fusion(bf16[1024,3072]{1,0:T(8,128)(2,1)} %get-tuple-element.337, f32[1024,768]{1,0:T(8,128)} %copy-done.19, f32[768]{0:T(1024)S(1)} %copy-done.87, f32[768]{0:T(1024)S(1)} %copy-done.73, f32[1024]{0:T(1024)S(1)} %fusion.191, f32[1024]{0:T(1024)S(1)} %broadcast_multiply_fusion.1), kind=kOutput, calls=%fused_computation.93 | convolution fusion | flops 4838129664 | bytes 14170112 | tf_op jit(solution)/shard_map/dot_general | solution.py:24
  282.8 8.9 %multiply_reduce_fusion.2 = (bf16[768]{0:T(1024)(128)(2,1)}, f32[1024]{0:T(1024)S(1)}, bf16[768]{0:T(1024)(128)(2,1)}, f32[1024,768]{1,0:T(8,128)S(1)}) fusion(f32[1024,768]{1,0:T(8,128)S(1)} %copy-done.20, f32[1024]{0:T(1024)S(1)} %fusion.191, f32[1024]{0:T(1024)S(1)} %broadcast_multiply_fusion.1, f32[768]{0:T(1024)S(1)} %copy-done.73, ...), kind=kOutput, calls=%fused_computation.116 | convolution fusion | flops 4839699456 | bytes 20469760 | tf_op jit(solution)/shard_map/dot_general | solution.py:30
  305.1 55.7 %while.27 = (s32[]{:T(128)}, f32[2,512,12,64]{1,3,2,0:T(8,128)}, bf16[2,512,12,64]{1,3,2,0:T(8,128)(2,1)}, f32[2,512,12,64]{1,3,2,0:T(8,128)}, bf16[2,512,12,64]...) while((s32[]{:T(128)}, f32[2,512,12,64]{1,3,2,0:T(8,128)}, ...), condition=%wide.region_20.21_spmd, body=%wide.region_18.20_spmd.sunk | while | flops 2061232640 | bytes 161414480 | solution.py:264
  309.8 7.3 multiply_reduce_fusion.9
  317.1 7.4 multiply_convert_fusion.3
  337.4 7.3 multiply_reduce_fusion.9
  344.7 7.4 multiply_convert_fusion.3
  424.1 10.6 %all-to-all-done.2 = bf16[8,256,256]{2,1,0:T(8,128)(2,1)} async-done(((bf16[8,256,256]{2,1,0:T(8,128)(2,1)}), bf16[8,256,256]{2,1,0:T(8,128)(2,1)}, u32[]{:S(2)}, u32[]{:S(2)}) %all-to-all-start.2) | async-done | bytes 1048608 | tf_op jit(solution)/shard_map/all_to_all | solution.py:305
  446.0 8.2 %fusion.60 = bf16[3840,256]{1,0:T(8,128)(2,1)} fusion(bf16[2048,256]{1,0:T(8,128)(2,1)} %bitcast.35, s32[2048]{0:T(1024)S(1)} %bitcast.722), kind=kOutput, calls=%fused_computation.89 | convolution fusion | flops 4035379200 | bytes 3022848 | tf_op jit(solution)/shard_map/dot_general | solution.py:20
  454.3 11.3 %all-to-all-done.3 = bf16[8,256,256]{2,1,0:T(8,128)(2,1)} async-done(((bf16[8,256,256]{2,1,0:T(8,128)(2,1)}), bf16[8,256,256]{2,1,0:T(8,128)(2,1)}, u32[]{:S(2)}, u32[]{:S(2)}) %all-to-all-start.3) | async-done | bytes 1048608 | tf_op jit(solution)/shard_map/all_to_all | solution.py:305
  474.0 7.2 fusion.61
  483.7 12.9 %all-to-all-done.4 = bf16[8,256,256]{2,1,0:T(8,128)(2,1)} async-done(((bf16[8,256,256]{2,1,0:T(8,128)(2,1)}), bf16[8,256,256]{2,1,0:T(8,128)(2,1)}, u32[]{:S(2)}, u32[]{:S(2)}) %all-to-all-start.4) | async-done | bytes 1048608 | tf_op jit(solution)/shard_map/all_to_all | solution.py:305
  496.6 7.5 fusion.62
  509.7 8.9 %collective-permute-done = bf16[2,480,256]{2,1,0:T(8,128)(2,1)S(1)} collective-permute-done((bf16[2,480,256]{2,1,0:T(8,128)(2,1)S(1)}, bf16[2,480,256]{2,1,0:T(8,128)(2,1)S(1)}, u32[]{:S(2)}, u32[]{:S(2)}) %collective-permute-start) | collective-permute-done | bytes 491552 | tf_op jit(solution)/shard_map/ppermute | solution.py:76
  520.3 7.5 collective-permute-done.8
  530.8 11.2 %collective-permute-done.16 = bf16[2,480,256]{2,1,0:T(8,128)(2,1)S(1)} collective-permute-done((bf16[2,480,256]{2,1,0:T(8,128)(2,1)S(1)}, bf16[2,480,256]{2,1,0:T(8,128)(2,1)S(1)}, u32[]{:S(2)}, u32[]{:S(2)}) %collective-permute-start.16) | collective-permute-done | bytes 491552 | tf_op jit(solution)/shard_map/ppermute | solution.py:76
  562.8 26.9 %collective-permute-done.6 = bf16[480,256]{1,0:T(8,128)(2,1)S(1)} collective-permute-done((bf16[480,256]{1,0:T(8,128)(2,1)S(1)}, bf16[480,256]{1,0:T(8,128)(2,1)S(1)}, u32[]{:S(2)}, u32[]{:S(2)}) %collective-permute-start.6) | collective-permute-done | bytes 245792 | tf_op jit(solution)/shard_map/ppermute | solution.py:76
  611.6 9.0 %collective-permute-done.49 = bf16[2,2,96,768]{3,2,0,1:T(8,128)(2,1)S(1)} collective-permute-done((bf16[2,2,96,768]{3,2,0,1:T(8,128)(2,1)S(1)}, bf16[2,2,96,768]{3,2,0,1:T(8,128)(2,1)S(1)}, u32[]{:S(2)}, u32[]{:S(2)}) %collective-permute-start.49) | collective-permute-done | bytes 589856 | tf_op jit(solution)/shard_map/ppermute | solution.py:76
  622.7 10.5 %collective-permute-done.37 = bf16[2,2,24,3072]{3,2,0,1:T(8,128)(2,1)S(1)} collective-permute-done((bf16[2,2,24,3072]{3,2,0,1:T(8,128)(2,1)S(1)}, bf16[2,2,24,3072]{3,2,0,1:T(8,128)(2,1)S(1)}, u32[]{:S(2)}, u32[]{:S(2)}) %collective-permute-start.37) | collective-permute-done | bytes 589856 | tf_op jit(solution)/shard_map/ppermute | solution.py:76
  639.1 23.7 %collective-permute-done.40 = bf16[2,24,3072]{2,1,0:T(8,128)(2,1)S(1)} collective-permute-done((bf16[2,24,3072]{2,1,0:T(8,128)(2,1)S(1)}, bf16[2,24,3072]{2,1,0:T(8,128)(2,1)S(1)}, u32[]{:S(2)}, u32[]{:S(2)}) %collective-permute-start.40) | collective-permute-done | bytes 294944 | tf_op jit(solution)/shard_map/ppermute | solution.py:76
  663.6 8.5 %collective-permute-done.38 = bf16[2,24,3072]{2,1,0:T(8,128)(2,1)S(1)} collective-permute-done((bf16[2,24,3072]{2,1,0:T(8,128)(2,1)S(1)}, bf16[2,24,3072]{2,1,0:T(8,128)(2,1)S(1)}, u32[]{:S(2)}, u32[]{:S(2)}) %collective-permute-start.38) | collective-permute-done | bytes 294944 | tf_op jit(solution)/shard_map/ppermute | solution.py:76
  674.4 7.7 collective-permute-done.50
  694.2 9.0 %collective-permute-done.19 = bf16[2,480,256]{2,1,0:T(8,128)(2,1)S(1)} collective-permute-done((bf16[2,480,256]{2,1,0:T(8,128)(2,1)S(1)}, bf16[2,480,256]{2,1,0:T(8,128)(2,1)S(1)}, u32[]{:S(2)}, u32[]{:S(2)}) %collective-permute-start.19) | collective-permute-done | bytes 491552 | tf_op jit(solution)/shard_map/ppermute | solution.py:76
  731.2 14.4 %collective-permute-done.47 = bf16[24,1536]{1,0:T(8,128)(2,1)S(1)} collective-permute-done((bf16[24,1536]{1,0:T(8,128)(2,1)S(1)}, bf16[24,1536]{1,0:T(8,128)(2,1)S(1)}, u32[]{:S(2)}, u32[]{:S(2)}) %collective-permute-start.47) | collective-permute-done | bytes 73760 | tf_op jit(solution)/shard_map/ppermute | solution.py:76
  (615 shorter events, 373.0 us)
Async XLA Ops:
  40.7 76.7 %all-to-all-start.1 = ((bf16[8,256,768]{2,1,0:T(8,128)(2,1)}), bf16[8,256,768]{2,1,0:T(8,128)(2,1)}, u32[]{:S(2)}, u32[]{:S(2)}) async-start(bf16[8,256,768]{2,1,0:T(8,128)(2,1)} %broadcast_select_fusion), calls=%async_computation.1 | async-start | bytes 6291456 | tf_op jit(solution)/shard_map/all_to_all | solution.py:212
  393.2 150.5 %collective-permute-start.48 = (bf16[4,384,768]{2,1,0:T(8,128)(2,1)}, bf16[4,384,768]{2,1,0:T(8,128)(2,1)}, u32[]{:S(2)}, u32[]{:S(2)}) collective-permute-start(bf16[4,384,768]{2,1,0:T(8,128)(2,1)} %dynamic-slice_bitcast_fusion.2), channel_id=1, source_target_pairs={{0,1},{1,0},{2,3},{3,2},{4,5},{5,4},{6,7},{7,6},{8,9},{9,8},{10,11... | collective-permute-start | bytes 7077896 | tf_op jit(solution)/shard_map/ppermute | solution.py:76
  394.9 152.7 %collective-permute-start.36 = (bf16[4,96,3072]{2,1,0:T(8,128)(2,1)}, bf16[4,96,3072]{2,1,0:T(8,128)(2,1)}, u32[]{:S(2)}, u32[]{:S(2)}) collective-permute-start(bf16[4,96,3072]{2,1,0:T(8,128)(2,1)} %dynamic-slice_bitcast_fusion.3), channel_id=1, source_target_pairs={{0,1},{1,0},{2,3},{3,2},{4,5},{5,4},{6,7},{7,6},{8,9},{9,8},{10,11... | collective-permute-start | bytes 7077896 | tf_op jit(solution)/shard_map/ppermute | solution.py:76
  403.7 31.0 %all-to-all-start.2 = ((bf16[8,256,256]{2,1,0:T(8,128)(2,1)}), bf16[8,256,256]{2,1,0:T(8,128)(2,1)}, u32[]{:S(2)}, u32[]{:S(2)}) async-start(bf16[8,256,256]{2,1,0:T(8,128)(2,1)} %bitcast.34), calls=%async_computation.2 | async-start | bytes 2097152 | tf_op jit(solution)/shard_map/all_to_all | solution.py:305
  434.7 30.8 %all-to-all-start.3 = ((bf16[8,256,256]{2,1,0:T(8,128)(2,1)}), bf16[8,256,256]{2,1,0:T(8,128)(2,1)}, u32[]{:S(2)}, u32[]{:S(2)}) async-start(bf16[8,256,256]{2,1,0:T(8,128)(2,1)} %bitcast.54), calls=%async_computation.3 | async-start | bytes 2097152 | tf_op jit(solution)/shard_map/all_to_all | solution.py:305
  445.7 189.6 %collective-permute-start.24 = (bf16[4,128,3072]{2,1,0:T(8,128)(2,1)}, bf16[4,128,3072]{2,1,0:T(8,128)(2,1)}, u32[]{:S(2)}, u32[]{:S(2)}) collective-permute-start(bf16[4,128,3072]{2,1,0:T(8,128)(2,1)} %dynamic-slice_bitcast_fusion.1), channel_id=1, source_target_pairs={{0,1},{1,0},{2,3},{3,2},{4,5},{5,4},{6,7},{7,6},{8,9},{9,8},{10,11... | collective-permute-start | bytes 9437192 | tf_op jit(solution)/shard_map/ppermute | solution.py:76
  465.5 31.1 %all-to-all-start.4 = ((bf16[8,256,256]{2,1,0:T(8,128)(2,1)}), bf16[8,256,256]{2,1,0:T(8,128)(2,1)}, u32[]{:S(2)}, u32[]{:S(2)}) async-start(bf16[8,256,256]{2,1,0:T(8,128)(2,1)} %bitcast.74), calls=%async_computation.4 | async-start | bytes 2097152 | tf_op jit(solution)/shard_map/all_to_all | solution.py:305
  472.5 31.9 %collective-permute-start.4 = (bf16[2,480,256]{2,1,0:T(8,128)(2,1)}, bf16[2,480,256]{2,1,0:T(8,128)(2,1)}, u32[]{:S(2)}, u32[]{:S(2)}) collective-permute-start(bf16[2,480,256]{2,1,0:T(8,128)(2,1)} %dynamic-slice_bitcast_fusion.9), channel_id=1, source_target_pairs={{0,16},{8,24},{16,0},{24,8},{1,17},{9,25},{17,1},{25,9},{2,18},{10... | collective-permute-start | bytes 1474568 | tf_op jit(solution)/shard_map/ppermute | solution.py:76
  483.2 24.0 %collective-permute-start.12 = (bf16[2,480,256]{2,1,0:T(8,128)(2,1)}, bf16[2,480,256]{2,1,0:T(8,128)(2,1)}, u32[]{:S(2)}, u32[]{:S(2)}) collective-permute-start(bf16[2,480,256]{2,1,0:T(8,128)(2,1)} %dynamic-slice_bitcast_fusion.7), channel_id=1, source_target_pairs={{0,16},{8,24},{16,0},{24,8},{1,17},{9,25},{17,1},{25,9},{2,18},{10... | collective-permute-start | bytes 1474568 | tf_op jit(solution)/shard_map/ppermute | solution.py:76
  504.4 14.2 %collective-permute-start = (bf16[2,480,256]{2,1,0:T(8,128)(2,1)S(1)}, bf16[2,480,256]{2,1,0:T(8,128)(2,1)S(1)}, u32[]{:S(2)}, u32[]{:S(2)}) collective-permute-start(bf16[2,480,256]{2,1,0:T(8,128)(2,1)S(1)} %dynamic-slice_bitcast_fusion.10), channel_id=1, source_target_pairs={{0,8},{8,0},{16,24},{24,16},{1,9},{9,1},{17,25},{25,17},{2,10},{10... | collective-permute-start | bytes 1474568 | tf_op jit(solution)/shard_map/ppermute | solution.py:76
  507.2 20.6 %collective-permute-start.8 = (bf16[2,480,256]{2,1,0:T(8,128)(2,1)S(1)}, bf16[2,480,256]{2,1,0:T(8,128)(2,1)S(1)}, u32[]{:S(2)}, u32[]{:S(2)}) collective-permute-start(bf16[2,480,256]{2,1,0:T(8,128)(2,1)S(1)} %dynamic-slice_bitcast_fusion.8), channel_id=1, source_target_pairs={{0,8},{8,0},{16,24},{24,16},{1,9},{9,1},{17,25},{25,17},{2,10},{10... | collective-permute-start | bytes 1474568 | tf_op jit(solution)/shard_map/ppermute | solution.py:76
  529.5 22.0 %collective-permute-start.5 = (bf16[480,256]{1,0:T(8,128)(2,1)S(1)}, bf16[480,256]{1,0:T(8,128)(2,1)S(1)}, u32[]{:S(2)}, u32[]{:S(2)}) collective-permute-start(bf16[480,256]{1,0:T(8,128)(2,1)S(1)} %dynamic-slice_bitcast_fusion.21), channel_id=1, source_target_pairs={{0,8},{8,0},{16,24},{24,16},{1,9},{9,1},{17,25},{25,17},{2,10},{10... | collective-permute-start | bytes 737288 | tf_op jit(solution)/shard_map/ppermute | solution.py:76
  553.9 56.0 %collective-permute-start.51 = (bf16[2,2,96,768]{3,2,0,1:T(8,128)(2,1)S(1)}, bf16[2,2,96,768]{3,2,0,1:T(8,128)(2,1)S(1)}, u32[]{:S(2)}, u32[]{:S(2)}) collective-permute-start(bf16[2,2,96,768]{3,2,0,1:T(8,128)(2,1)S(1)} %bitcast.717), channel_id=1, source_target_pairs={{0,16},{8,24},{16,0},{24,8},{1,17},{9,25},{17,1},{25,9},{2,18},{10... | collective-permute-start | bytes 1769480 | tf_op jit(solution)/shard_map/ppermute | solution.py:76
  556.6 53.6 %collective-permute-start.39 = (bf16[2,2,24,3072]{3,2,0,1:T(8,128)(2,1)S(1)}, bf16[2,2,24,3072]{3,2,0,1:T(8,128)(2,1)S(1)}, u32[]{:S(2)}, u32[]{:S(2)}) collective-permute-start(bf16[2,2,24,3072]{3,2,0,1:T(8,128)(2,1)S(1)} %bitcast.716), channel_id=1, source_target_pairs={{0,16},{8,24},{16,0},{24,8},{1,17},{9,25},{17,1},{25,9},{2,18},{10... | collective-permute-start | bytes 1769480 | tf_op jit(solution)/shard_map/ppermute | solution.py:76
  557.9 31.8 %collective-permute-start.6 = (bf16[480,256]{1,0:T(8,128)(2,1)S(1)}, bf16[480,256]{1,0:T(8,128)(2,1)S(1)}, u32[]{:S(2)}, u32[]{:S(2)}) collective-permute-start(bf16[480,256]{1,0:T(8,128)(2,1)S(1)} %fusion.133), channel_id=1, source_target_pairs={{0,16},{8,24},{16,0},{24,8},{1,17},{9,25},{17,1},{25,9},{2,18},{10... | collective-permute-start | bytes 737288 | tf_op jit(solution)/shard_map/ppermute | solution.py:76
  561.9 28.6 %collective-permute-start.2 = (bf16[480,256]{1,0:T(8,128)(2,1)S(1)}, bf16[480,256]{1,0:T(8,128)(2,1)S(1)}, u32[]{:S(2)}, u32[]{:S(2)}) collective-permute-start(bf16[480,256]{1,0:T(8,128)(2,1)S(1)} %fusion.134), channel_id=1, source_target_pairs={{0,8},{8,0},{16,24},{24,16},{1,9},{9,1},{17,25},{25,17},{2,10},{10... | collective-permute-start | bytes 737288 | tf_op jit(solution)/shard_map/ppermute | solution.py:76
  604.1 16.5 %collective-permute-start.49 = (bf16[2,2,96,768]{3,2,0,1:T(8,128)(2,1)S(1)}, bf16[2,2,96,768]{3,2,0,1:T(8,128)(2,1)S(1)}, u32[]{:S(2)}, u32[]{:S(2)}) collective-permute-start(bf16[2,2,96,768]{3,2,0,1:T(8,128)(2,1)S(1)} %bitcast.715), channel_id=1, source_target_pairs={{0,8},{8,0},{16,24},{24,16},{1,9},{9,1},{17,25},{25,17},{2,10},{10... | collective-permute-start | bytes 1769480 | tf_op jit(solution)/shard_map/ppermute | solution.py:76
  607.9 25.3 %collective-permute-start.37 = (bf16[2,2,24,3072]{3,2,0,1:T(8,128)(2,1)S(1)}, bf16[2,2,24,3072]{3,2,0,1:T(8,128)(2,1)S(1)}, u32[]{:S(2)}, u32[]{:S(2)}) collective-permute-start(bf16[2,2,24,3072]{3,2,0,1:T(8,128)(2,1)S(1)} %bitcast.714), channel_id=1, source_target_pairs={{0,8},{8,0},{16,24},{24,16},{1,9},{9,1},{17,25},{25,17},{2,10},{10... | collective-permute-start | bytes 1769480 | tf_op jit(solution)/shard_map/ppermute | solution.py:76
  609.9 76.1 %collective-permute-start.7 = (bf16[2,480,256]{2,1,0:T(8,128)(2,1)S(1)}, bf16[2,480,256]{2,1,0:T(8,128)(2,1)S(1)}, u32[]{:S(2)}, u32[]{:S(2)}) collective-permute-start(bf16[2,480,256]{2,1,0:T(8,128)(2,1)S(1)} %pad_maximum_fusion.5), channel_id=1, source_target_pairs={{0,8},{8,0},{16,24},{24,16},{1,9},{9,1},{17,25},{25,17},{2,10},{10... | collective-permute-start | bytes 1474568 | tf_op jit(solution)/shard_map/ppermute | solution.py:76
  610.3 73.6 %collective-permute-start.3 = (bf16[2,480,256]{2,1,0:T(8,128)(2,1)S(1)}, bf16[2,480,256]{2,1,0:T(8,128)(2,1)S(1)}, u32[]{:S(2)}, u32[]{:S(2)}) collective-permute-start(bf16[2,480,256]{2,1,0:T(8,128)(2,1)S(1)} %pad_maximum_fusion.4), channel_id=1, source_target_pairs={{0,16},{8,24},{16,0},{24,8},{1,17},{9,25},{17,1},{25,9},{2,18},{10... | collective-permute-start | bytes 1474568 | tf_op jit(solution)/shard_map/ppermute | solution.py:76
  620.6 72.6 %collective-permute-start.15 = (bf16[2,480,256]{2,1,0:T(8,128)(2,1)S(1)}, bf16[2,480,256]{2,1,0:T(8,128)(2,1)S(1)}, u32[]{:S(2)}, u32[]{:S(2)}) collective-permute-start(bf16[2,480,256]{2,1,0:T(8,128)(2,1)S(1)} %pad_maximum_fusion.7), channel_id=1, source_target_pairs={{0,8},{8,0},{16,24},{24,16},{1,9},{9,1},{17,25},{25,17},{2,10},{10... | collective-permute-start | bytes 1474568 | tf_op jit(solution)/shard_map/ppermute | solution.py:76
  633.2 40.1 %collective-permute-start.52 = (bf16[2,96,768]{2,1,0:T(8,128)(2,1)S(1)}, bf16[2,96,768]{2,1,0:T(8,128)(2,1)S(1)}, u32[]{:S(2)}, u32[]{:S(2)}) collective-permute-start(bf16[2,96,768]{2,1,0:T(8,128)(2,1)S(1)} %dynamic-slice_bitcast_fusion.13), channel_id=1, source_target_pairs={{0,8},{8,0},{16,24},{24,16},{1,9},{9,1},{17,25},{25,17},{2,10},{10... | collective-permute-start | bytes 884744 | tf_op jit(solution)/shard_map/ppermute | solution.py:76
  635.3 27.5 %collective-permute-start.40 = (bf16[2,24,3072]{2,1,0:T(8,128)(2,1)S(1)}, bf16[2,24,3072]{2,1,0:T(8,128)(2,1)S(1)}, u32[]{:S(2)}, u32[]{:S(2)}) collective-permute-start(bf16[2,24,3072]{2,1,0:T(8,128)(2,1)S(1)} %dynamic-slice_bitcast_fusion.15), channel_id=1, source_target_pairs={{0,8},{8,0},{16,24},{24,16},{1,9},{9,1},{17,25},{25,17},{2,10},{10... | collective-permute-start | bytes 884744 | tf_op jit(solution)/shard_map/ppermute | solution.py:76
  673.4 19.3 %collective-permute-start.11 = (bf16[2,480,256]{2,1,0:T(8,128)(2,1)S(1)}, bf16[2,480,256]{2,1,0:T(8,128)(2,1)S(1)}, u32[]{:S(2)}, u32[]{:S(2)}) collective-permute-start(bf16[2,480,256]{2,1,0:T(8,128)(2,1)S(1)} %pad_maximum_fusion.6), channel_id=1, source_target_pairs={{0,16},{8,24},{16,0},{24,8},{1,17},{9,25},{17,1},{25,9},{2,18},{10... | collective-permute-start | bytes 1474568 | tf_op jit(solution)/shard_map/ppermute | solution.py:76
  682.1 21.7 %collective-permute-start.23 = (bf16[2,480,256]{2,1,0:T(8,128)(2,1)S(1)}, bf16[2,480,256]{2,1,0:T(8,128)(2,1)S(1)}, u32[]{:S(2)}, u32[]{:S(2)}) collective-permute-start(bf16[2,480,256]{2,1,0:T(8,128)(2,1)S(1)} %pad_maximum_fusion.9), channel_id=1, source_target_pairs={{0,8},{8,0},{16,24},{24,16},{1,9},{9,1},{17,25},{25,17},{2,10},{10... | collective-permute-start | bytes 1474568 | tf_op jit(solution)/shard_map/ppermute | solution.py:76
  683.9 19.3 %collective-permute-start.19 = (bf16[2,480,256]{2,1,0:T(8,128)(2,1)S(1)}, bf16[2,480,256]{2,1,0:T(8,128)(2,1)S(1)}, u32[]{:S(2)}, u32[]{:S(2)}) collective-permute-start(bf16[2,480,256]{2,1,0:T(8,128)(2,1)S(1)} %pad_maximum_fusion.8), channel_id=1, source_target_pairs={{0,16},{8,24},{16,0},{24,8},{1,17},{9,25},{17,1},{25,9},{2,18},{10... | collective-permute-start | bytes 1474568 | tf_op jit(solution)/shard_map/ppermute | solution.py:76
  686.0 60.9 %collective-permute-start.27 = (bf16[2,2,32,3072]{3,2,1,0:T(8,128)(2,1)S(1)}, bf16[2,2,32,3072]{3,2,1,0:T(8,128)(2,1)S(1)}, u32[]{:S(2)}, u32[]{:S(2)}) collective-permute-start(bf16[2,2,32,3072]{3,2,1,0:T(8,128)(2,1)S(1)} %dynamic-slice_bitcast_fusion.4), channel_id=1, source_target_pairs={{0,16},{8,24},{16,0},{24,8},{1,17},{9,25},{17,1},{25,9},{2,18},{10... | collective-permute-start | bytes 2359304 | tf_op jit(solution)/shard_map/ppermute | solution.py:76
  692.6 22.6 %collective-permute-start.53 = (bf16[96,768]{1,0:T(8,128)(2,1)S(1)}, bf16[96,768]{1,0:T(8,128)(2,1)S(1)}, u32[]{:S(2)}, u32[]{:S(2)}) collective-permute-start(bf16[96,768]{1,0:T(8,128)(2,1)S(1)} %get-tuple-element.306), channel_id=1, source_target_pairs={{0,2},{1,3},{2,4},{3,5},{4,6},{5,7},{6,0},{7,1},{8,10},{9,11},{10,... | collective-permute-start | bytes 442376 | tf_op jit(solution)/shard_map/ppermute | solution.py:126
  727.8 19.4 %collective-permute-start.25 = (bf16[2,2,32,3072]{3,2,0,1:T(8,128)(2,1)S(1)}, bf16[2,2,32,3072]{3,2,0,1:T(8,128)(2,1)S(1)}, u32[]{:S(2)}, u32[]{:S(2)}) collective-permute-start(bf16[2,2,32,3072]{3,2,0,1:T(8,128)(2,1)S(1)} %bitcast.713), channel_id=1, source_target_pairs={{0,8},{8,0},{16,24},{24,16},{1,9},{9,1},{17,25},{25,17},{2,10},{10... | collective-permute-start | bytes 2359304 | tf_op jit(solution)/shard_map/ppermute | solution.py:76
  727.8 32.7 %collective-permute-start.57 = (bf16[96,384]{1,0:T(8,128)(2,1)S(1)}, bf16[96,384]{1,0:T(8,128)(2,1)S(1)}, u32[]{:S(2)}, u32[]{:S(2)}) collective-permute-start(bf16[96,384]{1,0:T(8,128)(2,1)S(1)} %slice.331), channel_id=1, source_target_pairs={{0,16},{8,24},{16,0},{24,8},{1,17},{9,25},{17,1},{25,9},{2,18},{10... | collective-permute-start | bytes 221192 | tf_op jit(solution)/shard_map/ppermute | solution.py:76
  729.0 31.5 %collective-permute-start.59 = (bf16[96,384]{1,0:T(8,128)(2,1)S(1)}, bf16[96,384]{1,0:T(8,128)(2,1)S(1)}, u32[]{:S(2)}, u32[]{:S(2)}) collective-permute-start(bf16[96,384]{1,0:T(8,128)(2,1)S(1)} %slice.332), channel_id=1, source_target_pairs={{0,8},{8,0},{16,24},{24,16},{1,9},{9,1},{17,25},{25,17},{2,10},{10... | collective-permute-start | bytes 221192 | tf_op jit(solution)/shard_map/ppermute | solution.py:76
  731.1 14.5 %collective-permute-start.47 = (bf16[24,1536]{1,0:T(8,128)(2,1)S(1)}, bf16[24,1536]{1,0:T(8,128)(2,1)S(1)}, u32[]{:S(2)}, u32[]{:S(2)}) collective-permute-start(bf16[24,1536]{1,0:T(8,128)(2,1)S(1)} %slice.327), channel_id=1, source_target_pairs={{0,8},{8,0},{16,24},{24,16},{1,9},{9,1},{17,25},{25,17},{2,10},{10... | collective-permute-start | bytes 221192 | tf_op jit(solution)/shard_map/ppermute | solution.py:76
  (143 other events, 1191.0 us)
where the time goes:
time: 790 us; the launch traced here: 786 us
  waiting for transfers between devices  292 us (37%)
  matrix products  200 us (25%)
  local copies, waits for them, and re-layouts  108 us (14%)
  other arithmetic  86.7 us (11%)
  starting transfers between devices  82.7 us (10%)
  blocking collectives  11.7 us (1%)
    ppermute x51, waiting for transfers between devices, swap(): return lax.ppermute(value, axis_name, [(i, i ^ bit) for i in range(size)])  176 us
    dot_general x10, matrix products, matmul(): return jnp.dot(left, right, preferred_element_type=jnp.float32)  78.2 us
    all_to_all x1, waiting for transfers between devices, local(): lax.all_to_all(found, 'vocab', split_axis=0, concat_axis=0, tiled=True)  69.1 us
    ppermute x51, starting transfers between devices, swap(): return lax.ppermute(value, axis_name, [(i, i ^ bit) for i in range(size)])  50.7 us
    dot_general x6, matrix products, matmul_nt(): lax.dot_general(left, right, (((1,), (1,)), ((), ())), preferred_element_...  35.4 us
    all_to_all x3, waiting for transfers between devices, local(): lax.all_to_all(outgoing[:, start:start + step].reshape(owners, capacity,...  34.8 us
    dot_general x6, matrix products, matmul_tn(): lax.dot_general(left, right, (((0,), (0,)), ((), ())), preferred_element_...  29.8 us
  transfers between devices with their start and end apart: 64, of which 34 were waited for; matrix products, arithmetic and copies ran while one was open for 11% of the time, Pallas kernels for 0%

commit v1 on v0

--- a/solution.py
+++ b/solution.py
@@ -302,13 +302,20 @@
     pieces = []
     step = 256
     for start in range(0, width, step):
-        incoming = lax.all_to_all(
-            outgoing[:, start : start + step].reshape(owners, capacity, step),
-            "vocab",
-            split_axis=0,
-            concat_axis=0,
-            tiled=True,
-        )
+        x = outgoing[:, start : start + step].reshape(owners, capacity, step)
+        ways, here = (lax.axis_size("vocab"), lax.axis_index("vocab"))
+        width_2 = x.shape[0] // ways
+        shape = list(x.shape)
+        shape[0] = width_2
+        height = shape[0]
+        shape[0] = height * ways
+        full = jnp.zeros(shape, x.dtype)
+        for mask in range(ways):
+            part = lax.dynamic_slice_in_dim(x, (here ^ mask) * width_2, width_2, axis=0)
+            if mask:
+                part = lax.ppermute(part, "vocab", [(d, d ^ mask) for d in range(ways)])
+            full = lax.dynamic_update_slice_in_dim(full, part, (here ^ mask) * height, axis=0)
+        incoming = full
         dense = matmul(hits, incoming.reshape(owners * capacity, step)).astype(bf)
         pieces.append(sum_over_dp(dense))
     grad_word = jnp.concatenate(pieces, 1)

time: 790 us -> 755 us (0.956)
  waiting for transfers between devices: 292 us -> 247 us
  starting transfers between devices: 82.7 us -> 109 us
  local copies, waits for them, and re-layouts: 108 us -> 98.6 us
    ppermute x51, waiting for transfers between devices: 176 us -> 123 us  [swap(): return lax.ppermute(value, axis_name, [(i, i ^ bit) for i in range(size)])]
    ppermute x0 -> x21, waiting for transfers between devices: none -> 42.1 us  [local(): part = lax.ppermute(part, 'vocab', [(d, d ^ mask) for d in range(ways)])]
    all_to_all x3 -> x0, waiting for transfers between devices: 34.8 us -> none  [local(): lax.all_to_all(outgoing[:, start:start + step].reshape(owners, capacity,...]
    ppermute x0 -> x21, starting transfers between devices: none -> 31.1 us  [local(): part = lax.ppermute(part, 'vocab', [(d, d ^ mask) for d in range(ways)])]
    all_to_all x3 -> x0, starting transfers between devices: 13.1 us -> none  [local(): lax.all_to_all(outgoing[:, start:start + step].reshape(owners, capacity,...]
    ppermute x51, starting transfers between devices: 50.7 us -> 59 us  [swap(): return lax.ppermute(value, axis_name, [(i, i ^ bit) for i in range(size)])]
  transfers between devices with their start and end apart: 64 -> 82, of which waited for: 34 -> 48; matrix products, arithmetic and copies ran while one was open for 11% -> 8% of each run, Pallas kernels for 0% -> 0%
where the time goes in v1:
time: 755 us; the launch traced here: 751 us
  waiting for transfers between devices  247 us (33%)
  matrix products  196 us (26%)
  starting transfers between devices  109 us (14%)
  local copies, waits for them, and re-layouts  98.6 us (13%)
  other arithmetic  83.4 us (11%)
  blocking collectives  11.7 us (2%)
    ppermute x51, waiting for transfers between devices, swap(): return lax.ppermute(value, axis_name, [(i, i ^ bit) for i in range(size)])  123 us
    dot_general x10, matrix products, matmul(): return jnp.dot(left, right, preferred_element_type=jnp.float32)  72.6 us
    all_to_all x1, waiting for transfers between devices, local(): lax.all_to_all(found, 'vocab', split_axis=0, concat_axis=0, tiled=True)  69.1 us
    ppermute x51, starting transfers between devices, swap(): return lax.ppermute(value, axis_name, [(i, i ^ bit) for i in range(size)])  59 us
    ppermute x21, waiting for transfers between devices, local(): part = lax.ppermute(part, 'vocab', [(d, d ^ mask) for d in range(ways)])  42.1 us
    dot_general x6, matrix products, matmul_nt(): lax.dot_general(left, right, (((1,), (1,)), ((), ())), preferred_element_...  35.2 us
    dot_general x6, matrix products, matmul_tn(): lax.dot_general(left, right, (((0,), (0,)), ((), ())), preferred_element_...  31.8 us
    ppermute x21, starting transfers between devices, local(): part = lax.ppermute(part, 'vocab', [(d, d ^ mask) for d in range(ways)])  31.1 us
  transfers between devices with their start and end apart: 82, of which 48 were waited for; matrix products, arithmetic and copies ran while one was open for 8% of the time, Pallas kernels for 0%

profile of v1, /device:TPU:0, one launch (start us, length us, event | category | flops | bytes accessed | tf_op | source)
XLA Modules:
  0.0 750.7 jit_solution(13133345940846752176)
XLA Ops:
  12.1 11.7 %all_to_all.14 = s32[8,1,256]{2,1,0:T(1,128)S(1)} all-to-all(s32[8,1,256]{2,1,0:T(1,128)S(1)} %bitcast.734), channel_id=1, replica_groups=mesh['dp'=4,'vocab'=8] {'vocab'}, dimensions={0} | all-to-all | bytes 16384 | tf_op jit(solution)/shard_map/all_to_all | solution.py:208
  23.9 13.5 %gather_fusion = bf16[2048,768]{1,0:T(8,128)(2,1)} fusion(bf16[3840,768]{1,0:T(8,128)(2,1)} %param.31, s32[2048]{0:T(1024)S(1)} %broadcast_clamp_fusion), kind=kCustom, calls=%fused_computation | custom fusion | bytes 6299648 | tf_op jit(solution)/shard_map/gather | solution.py:210
  48.2 69.1 %all-to-all-done.1 = bf16[8,256,768]{2,1,0:T(8,128)(2,1)} async-done(((bf16[8,256,768]{2,1,0:T(8,128)(2,1)}), bf16[8,256,768]{2,1,0:T(8,128)(2,1)}, u32[]{:S(2)}, u32[]{:S(2)}) %all-to-all-start.1) | async-done | bytes 3145760 | tf_op jit(solution)/shard_map/all_to_all | solution.py:212
  117.3 8.0 %gather_fusion.1 = bf16[1024,768]{1,0:T(8,128)(2,1)} fusion(bf16[2048,768]{1,0:T(8,128)(2,1)} %bitcast.25, s32[1024]{0:T(1024)S(1)} %broadcast_clamp_fusion.1), kind=kCustom, calls=%fused_computation.1 | custom fusion | bytes 3149824 | tf_op jit(solution)/shard_map/gather | solution.py:213
  164.1 25.6 %while.26 = (s32[]{:T(128)}, bf16[2,512,12,64]{1,3,2,0:T(8,128)(2,1)}, f32[2,12,512,1]{2,1,3,0:T(8,128)}, bf16[2,512,12,64]{1,3,2,0:T(8,128)(2,1)}, s32[2]{0:T(1...) while((s32[]{:T(128)}, ...), condition=%wide.region_9.10_spmd, body=%wide.region_6.9_spmd.sunk | while | flops 843442688 | bytes 47411840 | solution.py:236
  198.2 35.1 %multiply_convert_fusion.1 = (bf16[1024,3072]{1,0:T(8,128)(2,1)S(1)}, f32[1024,3072]{1,0:T(8,128)}, f32[1024,3072]{1,0:T(8,128)}) fusion(f32[3072]{0:T(1024)S(1)} %copy-done.75, bf16[768,3072]{1,0:T(8,128)(2,1)S(1)} %bitcast.744, f32[1024,768]{1,0:T(8,128)S(1)} %get-tuple-element.355, f32[768]{0:T(1024)S(1)} %copy-done.80, f32[768]{0:T(1024)S(1)} %copy-done.66, ...), kind=kOutput, calls=%fused_computation.69 | convolution fusion | flops 5043388416 | bytes 39348224 | tf_op jit(solution)/shard_map/dot_general | solution.py:20
  245.0 7.7 %convolution_convert_fusion = bf16[3072,768]{1,0:T(8,128)(2,1)} fusion(bf16[1024,3072]{1,0:T(8,128)(2,1)S(1)} %get-tuple-element.250, f32[1024,768]{1,0:T(8,128)S(1)} %get-tuple-element.249, f32[1024]{0:T(1024)S(1)} %negate_multiply_fusion.3), kind=kOutput, calls=%fused_computation.92 | convolution fusion | flops 4835770368 | bytes 14159872 | tf_op jit(solution)/shard_map/dot_general | solution.py:24
  252.7 19.4 %fusion.216 = (bf16[3072]{0:T(1024)(128)(2,1)}, bf16[1024,3072]{1,0:T(8,128)(2,1)}) fusion(f32[1024,3072]{1,0:T(8,128)} %get-tuple-element.251, bf16[3072,768]{1,0:T(8,128)(2,1)} %param.47, f32[1024,768]{1,0:T(8,128)} %copy-done.19, f32[1024]{0:T(1024)S(1)} %negate_multiply_fusion.3, f32[1024,3072]{1,0:T(8,128)} %get-tuple-element.356, f32[3072]{0:T(1024)S(1)} %copy-done.75), kind=kOutput, calls=%fused_computation.532 | convolution fusion | flops 4883739648 | bytes 39344128 | tf_op jit(solution)/shard_map/dot_general | solution.py:30
  272.1 10.7 %convolution_convert_fusion.1 = bf16[768,3072]{1,0:T(8,128)(2,1)} fusion(bf16[1024,3072]{1,0:T(8,128)(2,1)} %get-tuple-element.361, f32[1024,768]{1,0:T(8,128)} %copy-done.17, f32[768]{0:T(1024)S(1)} %copy-done.80, f32[768]{0:T(1024)S(1)} %copy-done.66, f32[1024]{0:T(1024)S(1)} %fusion.191, f32[1024]{0:T(1024)S(1)} %broadcast_multiply_fusion.1), kind=kOutput, calls=%fused_computation.93 | convolution fusion | flops 4838129664 | bytes 14170112 | tf_op jit(solution)/shard_map/dot_general | solution.py:24
  282.9 8.9 %multiply_reduce_fusion.2 = (bf16[768]{0:T(1024)(128)(2,1)}, f32[1024]{0:T(1024)S(1)}, bf16[768]{0:T(1024)(128)(2,1)}, f32[1024,768]{1,0:T(8,128)S(1)}) fusion(f32[1024,768]{1,0:T(8,128)S(1)} %copy-done.18, f32[1024]{0:T(1024)S(1)} %fusion.191, f32[1024]{0:T(1024)S(1)} %broadcast_multiply_fusion.1, f32[768]{0:T(1024)S(1)} %copy-done.66, ...), kind=kOutput, calls=%fused_computation.116 | convolution fusion | flops 4839699456 | bytes 20469760 | tf_op jit(solution)/shard_map/dot_general | solution.py:30
  305.3 56.1 %while.27 = (s32[]{:T(128)}, f32[2,512,12,64]{1,3,2,0:T(8,128)}, bf16[2,512,12,64]{1,3,2,0:T(8,128)(2,1)}, f32[2,512,12,64]{1,3,2,0:T(8,128)}, bf16[2,512,12,64]...) while((s32[]{:T(128)}, f32[2,512,12,64]{1,3,2,0:T(8,128)}, ...), condition=%wide.region_20.21_spmd, body=%wide.region_18.20_spmd.sunk | while | flops 2061232640 | bytes 161414480 | solution.py:264
  309.9 7.3 multiply_reduce_fusion.9
  317.2 7.4 multiply_convert_fusion.3
  337.6 7.3 multiply_reduce_fusion.9
  345.0 7.4 multiply_convert_fusion.3
  361.4 5.5 fusion.203
  423.7 5.9 collective-permute-done.1
  436.5 7.3 collective-permute-done.4
  450.0 6.0 fusion.60
  461.1 9.9 %collective-permute-done.18 = bf16[1,256,256]{2,1,0:T(8,128)(2,1)S(1)} collective-permute-done((bf16[1,256,256]{2,1,0:T(8,128)(2,1)S(1)}, bf16[1,256,256]{2,1,0:T(8,128)(2,1)S(1)}, u32[]{:S(2)}, u32[]{:S(2)}) %collective-permute-start.18) | collective-permute-done | bytes 131104 | tf_op jit(solution)/shard_map/ppermute | solution.py:316
  473.9 6.2 collective-permute-start.31
  482.5 6.0 fusion.61
  493.3 10.0 %collective-permute-done.33 = bf16[1,256,256]{2,1,0:T(8,128)(2,1)S(1)} collective-permute-done((bf16[1,256,256]{2,1,0:T(8,128)(2,1)S(1)}, bf16[1,256,256]{2,1,0:T(8,128)(2,1)S(1)}, u32[]{:S(2)}, u32[]{:S(2)}) %collective-permute-start.33) | collective-permute-done | bytes 131104 | tf_op jit(solution)/shard_map/ppermute | solution.py:316
  512.4 6.4 fusion.62
  521.7 8.1 %collective-permute-done.26 = bf16[2,480,256]{2,1,0:T(8,128)(2,1)S(1)} collective-permute-done((bf16[2,480,256]{2,1,0:T(8,128)(2,1)S(1)}, bf16[2,480,256]{2,1,0:T(8,128)(2,1)S(1)}, u32[]{:S(2)}, u32[]{:S(2)}) %collective-permute-start.26) | collective-permute-done | bytes 491552 | tf_op jit(solution)/shard_map/ppermute | solution.py:76
  534.0 8.2 %collective-permute-done.41 = bf16[2,480,256]{2,1,0:T(8,128)(2,1)S(1)} collective-permute-done((bf16[2,480,256]{2,1,0:T(8,128)(2,1)S(1)}, bf16[2,480,256]{2,1,0:T(8,128)(2,1)S(1)}, u32[]{:S(2)}, u32[]{:S(2)}) %collective-permute-start.41) | collective-permute-done | bytes 491552 | tf_op jit(solution)/shard_map/ppermute | solution.py:76
  590.8 8.7 %collective-permute-done.14 = bf16[2,480,256]{2,1,0:T(8,128)(2,1)S(1)} collective-permute-done((bf16[2,480,256]{2,1,0:T(8,128)(2,1)S(1)}, bf16[2,480,256]{2,1,0:T(8,128)(2,1)S(1)}, u32[]{:S(2)}, u32[]{:S(2)}) %collective-permute-start.14) | collective-permute-done | bytes 491552 | tf_op jit(solution)/shard_map/ppermute | solution.py:76
  601.3 11.1 %collective-permute-done.25 = bf16[2,480,256]{2,1,0:T(8,128)(2,1)S(1)} collective-permute-done((bf16[2,480,256]{2,1,0:T(8,128)(2,1)S(1)}, bf16[2,480,256]{2,1,0:T(8,128)(2,1)S(1)}, u32[]{:S(2)}, u32[]{:S(2)}) %collective-permute-start.25) | collective-permute-done | bytes 491552 | tf_op jit(solution)/shard_map/ppermute | solution.py:76
  616.8 6.4 collective-permute-done.40
  639.6 8.9 %collective-permute-done.72 = bf16[2,2,96,768]{3,2,0,1:T(8,128)(2,1)S(1)} collective-permute-done((bf16[2,2,96,768]{3,2,0,1:T(8,128)(2,1)S(1)}, bf16[2,2,96,768]{3,2,0,1:T(8,128)(2,1)S(1)}, u32[]{:S(2)}, u32[]{:S(2)}) %collective-permute-start.72) | collective-permute-done | bytes 589856 | tf_op jit(solution)/shard_map/ppermute | solution.py:76
  651.5 9.6 %collective-permute-done.60 = bf16[2,2,24,3072]{3,2,0,1:T(8,128)(2,1)S(1)} collective-permute-done((bf16[2,2,24,3072]{3,2,0,1:T(8,128)(2,1)S(1)}, bf16[2,2,24,3072]{3,2,0,1:T(8,128)(2,1)S(1)}, u32[]{:S(2)}, u32[]{:S(2)}) %collective-permute-start.60) | collective-permute-done | bytes 589856 | tf_op jit(solution)/shard_map/ppermute | solution.py:76
  701.4 7.8 %collective-permute-done.68 = bf16[24,1536]{1,0:T(8,128)(2,1)S(1)} collective-permute-done((bf16[24,1536]{1,0:T(8,128)(2,1)S(1)}, bf16[24,1536]{1,0:T(8,128)(2,1)S(1)}, u32[]{:S(2)}, u32[]{:S(2)}) %collective-permute-start.68) | collective-permute-done | bytes 73760 | tf_op jit(solution)/shard_map/ppermute | solution.py:76
  (664 shorter events, 400.9 us)
Async XLA Ops:
  40.7 76.6 %all-to-all-start.1 = ((bf16[8,256,768]{2,1,0:T(8,128)(2,1)}), bf16[8,256,768]{2,1,0:T(8,128)(2,1)}, u32[]{:S(2)}, u32[]{:S(2)}) async-start(bf16[8,256,768]{2,1,0:T(8,128)(2,1)} %broadcast_select_fusion), calls=%async_computation.1 | async-start | bytes 6291456 | tf_op jit(solution)/shard_map/all_to_all | solution.py:212
  403.3 226.0 %collective-permute-start.69 = (bf16[4,384,768]{2,1,0:T(8,128)(2,1)}, bf16[4,384,768]{2,1,0:T(8,128)(2,1)}, u32[]{:S(2)}, u32[]{:S(2)}) collective-permute-start(bf16[4,384,768]{2,1,0:T(8,128)(2,1)} %dynamic-slice_bitcast_fusion.2), channel_id=1, source_target_pairs={{0,1},{1,0},{2,3},{3,2},{4,5},{5,4},{6,7},{7,6},{8,9},{9,8},{10,11... | collective-permute-start | bytes 7077896 | tf_op jit(solution)/shard_map/ppermute | solution.py:76
  405.0 229.9 %collective-permute-start.57 = (bf16[4,96,3072]{2,1,0:T(8,128)(2,1)}, bf16[4,96,3072]{2,1,0:T(8,128)(2,1)}, u32[]{:S(2)}, u32[]{:S(2)}) collective-permute-start(bf16[4,96,3072]{2,1,0:T(8,128)(2,1)} %dynamic-slice_bitcast_fusion.3), channel_id=1, source_target_pairs={{0,1},{1,0},{2,3},{3,2},{4,5},{5,4},{6,7},{7,6},{8,9},{9,8},{10,11... | collective-permute-start | bytes 7077896 | tf_op jit(solution)/shard_map/ppermute | solution.py:76
  429.6 14.2 %collective-permute-start.4 = (bf16[1,256,256]{2,1,0:T(8,128)(2,1)S(1)}, bf16[1,256,256]{2,1,0:T(8,128)(2,1)S(1)}, u32[]{:S(2)}, u32[]{:S(2)}) collective-permute-start(bf16[1,256,256]{2,1,0:T(8,128)(2,1)S(1)} %get-tuple-element.297), channel_id=1, source_target_pairs={{0,5},{1,4},{2,7},{3,6},{4,1},{5,0},{6,3},{7,2},{8,13},{9,12},{10,... | collective-permute-start | bytes 393224 | tf_op jit(solution)/shard_map/ppermute | solution.py:316
  456.2 14.9 %collective-permute-start.18 = (bf16[1,256,256]{2,1,0:T(8,128)(2,1)S(1)}, bf16[1,256,256]{2,1,0:T(8,128)(2,1)S(1)}, u32[]{:S(2)}, u32[]{:S(2)}) collective-permute-start(bf16[1,256,256]{2,1,0:T(8,128)(2,1)S(1)} %get-tuple-element.306), channel_id=1, source_target_pairs={{0,4},{1,5},{2,6},{3,7},{4,0},{5,1},{6,2},{7,3},{8,12},{9,13},{10,... | collective-permute-start | bytes 393224 | tf_op jit(solution)/shard_map/ppermute | solution.py:316
  457.1 16.6 %collective-permute-start.19 = (bf16[1,256,256]{2,1,0:T(8,128)(2,1)S(1)}, bf16[1,256,256]{2,1,0:T(8,128)(2,1)S(1)}, u32[]{:S(2)}, u32[]{:S(2)}) collective-permute-start(bf16[1,256,256]{2,1,0:T(8,128)(2,1)S(1)} %get-tuple-element.305), channel_id=1, source_target_pairs={{0,5},{1,4},{2,7},{3,6},{4,1},{5,0},{6,3},{7,2},{8,13},{9,12},{10,... | collective-permute-start | bytes 393224 | tf_op jit(solution)/shard_map/ppermute | solution.py:316
  458.8 15.1 %collective-permute-start.20 = (bf16[1,256,256]{2,1,0:T(8,128)(2,1)S(1)}, bf16[1,256,256]{2,1,0:T(8,128)(2,1)S(1)}, u32[]{:S(2)}, u32[]{:S(2)}) collective-permute-start(bf16[1,256,256]{2,1,0:T(8,128)(2,1)S(1)} %get-tuple-element.304), channel_id=1, source_target_pairs={{0,6},{1,7},{2,4},{3,5},{4,2},{5,3},{6,0},{7,1},{8,14},{9,15},{10,... | collective-permute-start | bytes 393224 | tf_op jit(solution)/shard_map/ppermute | solution.py:316
  473.7 14.9 %collective-permute-start.30 = (bf16[1,256,256]{2,1,0:T(8,128)(2,1)S(1)}, bf16[1,256,256]{2,1,0:T(8,128)(2,1)S(1)}, u32[]{:S(2)}, u32[]{:S(2)}) collective-permute-start(bf16[1,256,256]{2,1,0:T(8,128)(2,1)S(1)} %get-tuple-element.317), channel_id=1, source_target_pairs={{0,1},{1,0},{2,3},{3,2},{4,5},{5,4},{6,7},{7,6},{8,9},{9,8},{10,11... | collective-permute-start | bytes 393224 | tf_op jit(solution)/shard_map/ppermute | solution.py:316
  473.9 15.4 %collective-permute-start.31 = (bf16[1,256,256]{2,1,0:T(8,128)(2,1)S(1)}, bf16[1,256,256]{2,1,0:T(8,128)(2,1)S(1)}, u32[]{:S(2)}, u32[]{:S(2)}) collective-permute-start(bf16[1,256,256]{2,1,0:T(8,128)(2,1)S(1)} %get-tuple-element.316), channel_id=1, source_target_pairs={{0,2},{1,3},{2,0},{3,1},{4,6},{5,7},{6,4},{7,5},{8,10},{9,11},{10,... | collective-permute-start | bytes 393224 | tf_op jit(solution)/shard_map/ppermute | solution.py:316
  488.7 14.7 %collective-permute-start.33 = (bf16[1,256,256]{2,1,0:T(8,128)(2,1)S(1)}, bf16[1,256,256]{2,1,0:T(8,128)(2,1)S(1)}, u32[]{:S(2)}, u32[]{:S(2)}) collective-permute-start(bf16[1,256,256]{2,1,0:T(8,128)(2,1)S(1)} %get-tuple-element.314), channel_id=1, source_target_pairs={{0,4},{1,5},{2,6},{3,7},{4,0},{5,1},{6,2},{7,3},{8,12},{9,13},{10,... | collective-permute-start | bytes 393224 | tf_op jit(solution)/shard_map/ppermute | solution.py:316
  489.3 16.8 %collective-permute-start.34 = (bf16[1,256,256]{2,1,0:T(8,128)(2,1)S(1)}, bf16[1,256,256]{2,1,0:T(8,128)(2,1)S(1)}, u32[]{:S(2)}, u32[]{:S(2)}) collective-permute-start(bf16[1,256,256]{2,1,0:T(8,128)(2,1)S(1)} %get-tuple-element.313), channel_id=1, source_target_pairs={{0,5},{1,4},{2,7},{3,6},{4,1},{5,0},{6,3},{7,2},{8,13},{9,12},{10,... | collective-permute-start | bytes 393224 | tf_op jit(solution)/shard_map/ppermute | solution.py:316
  491.5 16.1 %collective-permute-start.35 = (bf16[1,256,256]{2,1,0:T(8,128)(2,1)S(1)}, bf16[1,256,256]{2,1,0:T(8,128)(2,1)S(1)}, u32[]{:S(2)}, u32[]{:S(2)}) collective-permute-start(bf16[1,256,256]{2,1,0:T(8,128)(2,1)S(1)} %get-tuple-element.312), channel_id=1, source_target_pairs={{0,6},{1,7},{2,4},{3,5},{4,2},{5,3},{6,0},{7,1},{8,14},{9,15},{10,... | collective-permute-start | bytes 393224 | tf_op jit(solution)/shard_map/ppermute | solution.py:316
  506.0 14.1 %collective-permute-start.11 = (bf16[2,480,256]{2,1,0:T(8,128)(2,1)S(1)}, bf16[2,480,256]{2,1,0:T(8,128)(2,1)S(1)}, u32[]{:S(2)}, u32[]{:S(2)}) collective-permute-start(bf16[2,480,256]{2,1,0:T(8,128)(2,1)S(1)} %dynamic-slice_bitcast_fusion.9), channel_id=1, source_target_pairs={{0,16},{8,24},{16,0},{24,8},{1,17},{9,25},{17,1},{25,9},{2,18},{10... | collective-permute-start | bytes 1474568 | tf_op jit(solution)/shard_map/ppermute | solution.py:76
  507.6 23.8 %collective-permute-start.7 = (bf16[2,480,256]{2,1,0:T(8,128)(2,1)S(1)}, bf16[2,480,256]{2,1,0:T(8,128)(2,1)S(1)}, u32[]{:S(2)}, u32[]{:S(2)}) collective-permute-start(bf16[2,480,256]{2,1,0:T(8,128)(2,1)S(1)} %dynamic-slice_bitcast_fusion.10), channel_id=1, source_target_pairs={{0,8},{8,0},{16,24},{24,16},{1,9},{9,1},{17,25},{25,17},{2,10},{10... | collective-permute-start | bytes 1474568 | tf_op jit(solution)/shard_map/ppermute | solution.py:76
  510.8 19.0 %collective-permute-start.26 = (bf16[2,480,256]{2,1,0:T(8,128)(2,1)S(1)}, bf16[2,480,256]{2,1,0:T(8,128)(2,1)S(1)}, u32[]{:S(2)}, u32[]{:S(2)}) collective-permute-start(bf16[2,480,256]{2,1,0:T(8,128)(2,1)S(1)} %dynamic-slice_bitcast_fusion.7), channel_id=1, source_target_pairs={{0,16},{8,24},{16,0},{24,8},{1,17},{9,25},{17,1},{25,9},{2,18},{10... | collective-permute-start | bytes 1474568 | tf_op jit(solution)/shard_map/ppermute | solution.py:76
  520.1 13.2 %collective-permute-start.22 = (bf16[2,480,256]{2,1,0:T(8,128)(2,1)S(1)}, bf16[2,480,256]{2,1,0:T(8,128)(2,1)S(1)}, u32[]{:S(2)}, u32[]{:S(2)}) collective-permute-start(bf16[2,480,256]{2,1,0:T(8,128)(2,1)S(1)} %dynamic-slice_bitcast_fusion.8), channel_id=1, source_target_pairs={{0,8},{8,0},{16,24},{24,16},{1,9},{9,1},{17,25},{25,17},{2,10},{10... | collective-permute-start | bytes 1474568 | tf_op jit(solution)/shard_map/ppermute | solution.py:76
  531.5 14.2 %collective-permute-start.37 = (bf16[2,480,256]{2,1,0:T(8,128)(2,1)S(1)}, bf16[2,480,256]{2,1,0:T(8,128)(2,1)S(1)}, u32[]{:S(2)}, u32[]{:S(2)}) collective-permute-start(bf16[2,480,256]{2,1,0:T(8,128)(2,1)S(1)} %dynamic-slice_bitcast_fusion.6), channel_id=1, source_target_pairs={{0,8},{8,0},{16,24},{24,16},{1,9},{9,1},{17,25},{25,17},{2,10},{10... | collective-permute-start | bytes 1474568 | tf_op jit(solution)/shard_map/ppermute | solution.py:76
  533.3 17.7 %collective-permute-start.12 = (bf16[480,256]{1,0:T(8,128)(2,1)S(1)}, bf16[480,256]{1,0:T(8,128)(2,1)S(1)}, u32[]{:S(2)}, u32[]{:S(2)}) collective-permute-start(bf16[480,256]{1,0:T(8,128)(2,1)S(1)} %dynamic-slice_bitcast_fusion.21), channel_id=1, source_target_pairs={{0,8},{8,0},{16,24},{24,16},{1,9},{9,1},{17,25},{25,17},{2,10},{10... | collective-permute-start | bytes 737288 | tf_op jit(solution)/shard_map/ppermute | solution.py:76
  575.7 13.1 %collective-permute-start.10 = (bf16[2,480,256]{2,1,0:T(8,128)(2,1)S(1)}, bf16[2,480,256]{2,1,0:T(8,128)(2,1)S(1)}, u32[]{:S(2)}, u32[]{:S(2)}) collective-permute-start(bf16[2,480,256]{2,1,0:T(8,128)(2,1)S(1)} %pad_maximum_fusion.4), channel_id=1, source_target_pairs={{0,16},{8,24},{16,0},{24,8},{1,17},{9,25},{17,1},{25,9},{2,18},{10... | collective-permute-start | bytes 1474568 | tf_op jit(solution)/shard_map/ppermute | solution.py:76
  580.9 83.2 %collective-permute-start.45 = (bf16[4,128,3072]{2,1,0:T(8,128)(2,1)S(1)}, bf16[4,128,3072]{2,1,0:T(8,128)(2,1)S(1)}, u32[]{:S(2)}, u32[]{:S(2)}) collective-permute-start(bf16[4,128,3072]{2,1,0:T(8,128)(2,1)S(1)} %dynamic-slice_bitcast_fusion.1), channel_id=1, source_target_pairs={{0,1},{1,0},{2,3},{3,2},{4,5},{5,4},{6,7},{7,6},{8,9},{9,8},{10,11... | collective-permute-start | bytes 9437192 | tf_op jit(solution)/shard_map/ppermute | solution.py:76
  585.4 14.2 %collective-permute-start.14 = (bf16[2,480,256]{2,1,0:T(8,128)(2,1)S(1)}, bf16[2,480,256]{2,1,0:T(8,128)(2,1)S(1)}, u32[]{:S(2)}, u32[]{:S(2)}) collective-permute-start(bf16[2,480,256]{2,1,0:T(8,128)(2,1)S(1)} %pad_maximum_fusion.5), channel_id=1, source_target_pairs={{0,8},{8,0},{16,24},{24,16},{1,9},{9,1},{17,25},{25,17},{2,10},{10... | collective-permute-start | bytes 1474568 | tf_op jit(solution)/shard_map/ppermute | solution.py:76
  588.8 25.5 %collective-permute-start.29 = (bf16[2,480,256]{2,1,0:T(8,128)(2,1)S(1)}, bf16[2,480,256]{2,1,0:T(8,128)(2,1)S(1)}, u32[]{:S(2)}, u32[]{:S(2)}) collective-permute-start(bf16[2,480,256]{2,1,0:T(8,128)(2,1)S(1)} %pad_maximum_fusion.7), channel_id=1, source_target_pairs={{0,8},{8,0},{16,24},{24,16},{1,9},{9,1},{17,25},{25,17},{2,10},{10... | collective-permute-start | bytes 1474568 | tf_op jit(solution)/shard_map/ppermute | solution.py:76
  632.2 16.3 %collective-permute-start.72 = (bf16[2,2,96,768]{3,2,0,1:T(8,128)(2,1)S(1)}, bf16[2,2,96,768]{3,2,0,1:T(8,128)(2,1)S(1)}, u32[]{:S(2)}, u32[]{:S(2)}) collective-permute-start(bf16[2,2,96,768]{3,2,0,1:T(8,128)(2,1)S(1)} %bitcast.721), channel_id=1, source_target_pairs={{0,16},{8,24},{16,0},{24,8},{1,17},{9,25},{17,1},{25,9},{2,18},{10... | collective-permute-start | bytes 1769480 | tf_op jit(solution)/shard_map/ppermute | solution.py:76
  634.3 16.3 %collective-permute-start.70 = (bf16[2,2,96,768]{3,2,0,1:T(8,128)(2,1)S(1)}, bf16[2,2,96,768]{3,2,0,1:T(8,128)(2,1)S(1)}, u32[]{:S(2)}, u32[]{:S(2)}) collective-permute-start(bf16[2,2,96,768]{3,2,0,1:T(8,128)(2,1)S(1)} %bitcast.720), channel_id=1, source_target_pairs={{0,8},{8,0},{16,24},{24,16},{1,9},{9,1},{17,25},{25,17},{2,10},{10... | collective-permute-start | bytes 1769480 | tf_op jit(solution)/shard_map/ppermute | solution.py:76
  637.8 23.3 %collective-permute-start.60 = (bf16[2,2,24,3072]{3,2,0,1:T(8,128)(2,1)S(1)}, bf16[2,2,24,3072]{3,2,0,1:T(8,128)(2,1)S(1)}, u32[]{:S(2)}, u32[]{:S(2)}) collective-permute-start(bf16[2,2,24,3072]{3,2,0,1:T(8,128)(2,1)S(1)} %bitcast.723), channel_id=1, source_target_pairs={{0,16},{8,24},{16,0},{24,8},{1,17},{9,25},{17,1},{25,9},{2,18},{10... | collective-permute-start | bytes 1769480 | tf_op jit(solution)/shard_map/ppermute | solution.py:76
  638.1 23.8 %collective-permute-start.58 = (bf16[2,2,24,3072]{3,2,0,1:T(8,128)(2,1)S(1)}, bf16[2,2,24,3072]{3,2,0,1:T(8,128)(2,1)S(1)}, u32[]{:S(2)}, u32[]{:S(2)}) collective-permute-start(bf16[2,2,24,3072]{3,2,0,1:T(8,128)(2,1)S(1)} %bitcast.722), channel_id=1, source_target_pairs={{0,8},{8,0},{16,24},{24,16},{1,9},{9,1},{17,25},{25,17},{2,10},{10... | collective-permute-start | bytes 1769480 | tf_op jit(solution)/shard_map/ppermute | solution.py:76
  648.7 25.5 %collective-permute-start.73 = (bf16[2,96,768]{2,1,0:T(8,128)(2,1)S(1)}, bf16[2,96,768]{2,1,0:T(8,128)(2,1)S(1)}, u32[]{:S(2)}, u32[]{:S(2)}) collective-permute-start(bf16[2,96,768]{2,1,0:T(8,128)(2,1)S(1)} %dynamic-slice_bitcast_fusion.13), channel_id=1, source_target_pairs={{0,8},{8,0},{16,24},{24,16},{1,9},{9,1},{17,25},{25,17},{2,10},{10... | collective-permute-start | bytes 884744 | tf_op jit(solution)/shard_map/ppermute | solution.py:76
  650.8 26.3 %collective-permute-start.71 = (bf16[2,96,768]{2,1,0:T(8,128)(2,1)S(1)}, bf16[2,96,768]{2,1,0:T(8,128)(2,1)S(1)}, u32[]{:S(2)}, u32[]{:S(2)}) collective-permute-start(bf16[2,96,768]{2,1,0:T(8,128)(2,1)S(1)} %dynamic-slice_bitcast_fusion.14), channel_id=1, source_target_pairs={{0,16},{8,24},{16,0},{24,8},{1,17},{9,25},{17,1},{25,9},{2,18},{10... | collective-permute-start | bytes 884744 | tf_op jit(solution)/shard_map/ppermute | solution.py:76
  665.7 44.7 %collective-permute-start.48 = (bf16[2,2,32,3072]{3,2,1,0:T(8,128)(2,1)S(1)}, bf16[2,2,32,3072]{3,2,1,0:T(8,128)(2,1)S(1)}, u32[]{:S(2)}, u32[]{:S(2)}) collective-permute-start(bf16[2,2,32,3072]{3,2,1,0:T(8,128)(2,1)S(1)} %dynamic-slice_bitcast_fusion.4), channel_id=1, source_target_pairs={{0,16},{8,24},{16,0},{24,8},{1,17},{9,25},{17,1},{25,9},{2,18},{10... | collective-permute-start | bytes 2359304 | tf_op jit(solution)/shard_map/ppermute | solution.py:76
  695.6 16.6 %collective-permute-start.46 = (bf16[2,2,32,3072]{3,2,0,1:T(8,128)(2,1)S(1)}, bf16[2,2,32,3072]{3,2,0,1:T(8,128)(2,1)S(1)}, u32[]{:S(2)}, u32[]{:S(2)}) collective-permute-start(bf16[2,2,32,3072]{3,2,0,1:T(8,128)(2,1)S(1)} %bitcast.719), channel_id=1, source_target_pairs={{0,8},{8,0},{16,24},{24,16},{1,9},{9,1},{17,25},{25,17},{2,10},{10... | collective-permute-start | bytes 2359304 | tf_op jit(solution)/shard_map/ppermute | solution.py:76
  697.0 28.9 %collective-permute-start.78 = (bf16[96,384]{1,0:T(8,128)(2,1)S(1)}, bf16[96,384]{1,0:T(8,128)(2,1)S(1)}, u32[]{:S(2)}, u32[]{:S(2)}) collective-permute-start(bf16[96,384]{1,0:T(8,128)(2,1)S(1)} %slice.331), channel_id=1, source_target_pairs={{0,16},{8,24},{16,0},{24,8},{1,17},{9,25},{17,1},{25,9},{2,18},{10... | collective-permute-start | bytes 221192 | tf_op jit(solution)/shard_map/ppermute | solution.py:76
  699.3 26.7 %collective-permute-start.80 = (bf16[96,384]{1,0:T(8,128)(2,1)S(1)}, bf16[96,384]{1,0:T(8,128)(2,1)S(1)}, u32[]{:S(2)}, u32[]{:S(2)}) collective-permute-start(bf16[96,384]{1,0:T(8,128)(2,1)S(1)} %slice.332), channel_id=1, source_target_pairs={{0,8},{8,0},{16,24},{24,16},{1,9},{9,1},{17,25},{25,17},{2,10},{10... | collective-permute-start | bytes 221192 | tf_op jit(solution)/shard_map/ppermute | solution.py:76
  (154 other events, 1195.8 us)
